TPU v7x, 512 devices: a whole 4x8x8 slice. The times are simulated.
512 devices in a mesh: vox: 32 (over z_lo, y), opt: 16 (over z_hi, x, core).
Axes of the slice: x: 4, y: 8, z: 8 (z_hi: 2, z_lo: 4; z = z_hi * 4 + z_lo), core: 2. Of those that a mesh axis runs over, the one named last changes fastest.
Arguments:
- source_fields: bfloat16 [1024, 24576], P('opt', 'vox'), may hold values from -6 to 6
- detector_fields: bfloat16 [4096, 24576], P('opt', 'vox'), may hold values from -6 to 6
- measured: float32 [1024, 4096], P('vox', 'opt'), may hold values from -6 to 6
- valid_pair: int32 [1024, 4096], P('vox', 'opt'), may hold values 0 or 1
- weight_class: int32 [1024, 4096], P('vox', 'opt'), may hold values from 0 to 3
- absorption: float32 [24576], P('vox'), may hold values from 0 to 1
Outputs:
- absorption_out: float32 [24576], P('vox')
- residual_out: float32 [1024, 4096], P('vox', 'opt')
All inputs are finite; a program needn't handle non-finite values. No bound on the sum of `valid_pair` on one device may be relied on, other than what follows from the above.
Results may differ from a plain program's by a relative error of at most 0.0026.
Values may be sent and summed in bfloat16 or wider, within the bound.
No kernel may reach another device: no remote copies, remote signals or barrier semaphores. Data moves between devices by JAX's collectives and lax.ppermute only.
A program may use at most 64 MiB of HBM per device.

v0:
```python
import jax
import jax.numpy as jnp
from jax import lax
from jax.sharding import PartitionSpec as P

NS = 1024
ND = 4096
ITERS = 2


def local(source_fields, detector_fields, measured, valid_pair, weight_class, absorption):
    vox_count = lax.axis_size("vox")
    voxels = absorption.shape[0] * vox_count
    pred_scale = 1.0 / jnp.sqrt(jnp.float32(voxels))
    grad_scale = jnp.sqrt(jnp.float32(voxels)) / (jnp.float32(NS) * jnp.float32(ND))
    own_rows = measured.shape[0]
    maskf = valid_pair.astype(jnp.float32) / (1.0 + weight_class.astype(jnp.float32))
    mu_now = absorption
    weighted = jnp.zeros(measured.shape, jnp.float32)
    for step in range(ITERS):
        scaled = (detector_fields * mu_now[None, :]).astype(jnp.bfloat16)
        partial_pred = lax.dot_general(
            lax.all_gather(source_fields, "opt", axis=0, tiled=True),
            scaled,
            (((1,), (1,)), ((), ())),
            preferred_element_type=jnp.float32,
        )
        summed = lax.psum(partial_pred, "vox")
        predicted = lax.dynamic_slice_in_dim(summed, lax.axis_index("vox") * own_rows, own_rows, 0)
        weighted = maskf * (predicted * pred_scale - measured)
        weighted_b = weighted.astype(jnp.bfloat16)
        inner = jnp.dot(
            lax.all_gather(weighted_b, "vox", axis=0, tiled=True),
            detector_fields,
            preferred_element_type=jnp.float32,
        )
        local_grad = jnp.sum(
            inner * lax.all_gather(source_fields, "opt", axis=0, tiled=True), axis=0
        )
        gradient = lax.psum(local_grad, "opt") * grad_scale
        mu_now = jnp.maximum(mu_now - 2.0 * gradient, 0.0)
    return (mu_now, weighted)


def solution(mesh):
    placed = (
        P("opt", "vox"),
        P("opt", "vox"),
        P("vox", "opt"),
        P("vox", "opt"),
        P("vox", "opt"),
        P("vox"),
    )
    return jax.shard_map(
        local, mesh=mesh, in_specs=placed, out_specs=(P("vox"), P("vox", "opt")), check_vma=False
    )
```

profile of v0, /device:TPU:1, one launch (start us, length us, event | category | flops | bytes accessed | tf_op | source)
XLA Modules:
  0.0 953.0 jit_solution(11896403717239012675)
XLA Ops:
  7.2 0.0 all-gather.2.cloned.1.call-start
  7.2 0.7 all-gather.2.cloned.1.call-update
  7.9 0.0 copy-start.2
  7.9 0.0 copy-start.3
  7.9 0.0 copy-start.4
  7.9 0.0 all-reduce.3.cloned.1.call-start
  8.0 74.2 %all-gather.2.cloned.1.call-done = bf16[1024,768]{1,0:T(8,128)(2,1)} async-done(((bf16[64,768]{1,0:T(8,128)(2,1)}), bf16[1024,768]{1,0:T(8,128)(2,1)}) %all-gather.2.cloned.1.call-update) | async-done | bytes 1572880 | tf_op jit(solution)/shard_map/all_gather | solution.py:23
  82.2 0.0 copy-start.1
  82.2 3.2 convolution_bitcast_fusion.1
  85.4 0.0 copy-start
  85.4 0.0 all-reduce.3.cloned.1.call-update
  85.4 0.0 all-reduce.5.cloned.1.call-start
  85.5 284.5 %all-reduce.3.cloned.1.call-done = f32[1024,256]{1,0:T(8,128)} async-done(((f32[1024,256]{1,0:T(8,128)}), f32[1024,256]{1,0:T(8,128)}) %all-reduce.3.cloned.1.call-update) | async-done | bytes 1048592 | tf_op jit(solution)/shard_map/psum | solution.py:28
  370.0 0.0 copy-done.2
  370.0 0.0 copy-done.3
  370.0 0.0 copy-done.4
  370.0 0.8 multiply_convert_fusion
  370.8 66.8 %all_gather.13 = bf16[1024,256]{1,0:T(8,128)(2,1)S(1)} all-gather(bf16[32,256]{1,0:T(8,128)(2,1)S(1)} %multiply_convert_fusion), channel_id=1, replica_groups=mesh['vox'=32,'opt'=16] {'vox'}, dimensions={0}, use_global_device_ids=true | all-gather | bytes 540672 | tf_op jit(solution)/shard_map/all_gather | solution.py:33
  437.6 0.0 copy-done.1
  437.6 0.0 copy-done
  437.6 0.0 copy-start.5
  437.6 0.6 fusion
  438.2 78.6 %psum.29 = f32[768]{0:T(1024)S(1)} all-reduce(f32[768]{0:T(1024)S(1)} %fusion), channel_id=1, replica_groups=mesh['vox'=32,'opt'=16] {'opt'}, use_global_device_ids=true, to_apply=%region_2.0 | all-reduce | flops 768 | bytes 6144 | tf_op jit(solution)/shard_map/psum | solution.py:40
  516.8 0.0 copy-done.5
  516.8 1.6 convolution_bitcast_fusion
  518.5 0.0 all-reduce.5.cloned.1.call-update
  518.5 280.0 %all-reduce.5.cloned.1.call-done = f32[1024,256]{1,0:T(8,128)} async-done(((f32[1024,256]{1,0:T(8,128)}), f32[1024,256]{1,0:T(8,128)}) %all-reduce.5.cloned.1.call-update) | async-done | bytes 1048592 | tf_op jit(solution)/shard_map/psum | solution.py:28
  798.5 1.4 fusion.8
  799.9 65.8 %all_gather.14 = bf16[1024,256]{1,0:T(8,128)(2,1)S(1)} all-gather(bf16[32,256]{1,0:T(8,128)(2,1)S(1)} %get-tuple-element.6), channel_id=1, replica_groups=mesh['vox'=32,'opt'=16] {'vox'}, dimensions={0}, use_global_device_ids=true | all-gather | bytes 540672 | tf_op jit(solution)/shard_map/all_gather | solution.py:33
  865.7 0.6 fusion.1
  866.4 79.5 %psum.31 = f32[768]{0:T(1024)S(1)} all-reduce(f32[768]{0:T(1024)S(1)} %fusion.1), channel_id=1, replica_groups=mesh['vox'=32,'opt'=16] {'opt'}, use_global_device_ids=true, to_apply=%region_5.0 | all-reduce | flops 768 | bytes 6144 | tf_op jit(solution)/shard_map/psum | solution.py:40
  945.8 0.6 subtract_maximum_fusion
  (1 shorter events, 0.0 us)
Async XLA Ops:
  7.2 75.0 %all-gather.2.cloned.1.call-start = ((), (), s32[]{:S(2)}) async-start(), calls=%async_computation | async-start | bytes 1671168 | tf_op jit(solution)/shard_map/all_gather | solution.py:23
  7.9 362.1 %copy-start.2 = (f32[32,256]{1,0:T(8,128)S(1)}, f32[32,256]{1,0:T(8,128)}, u32[]{:S(2)}) copy-start(f32[32,256]{1,0:T(8,128)} %param.8) | copy-start | bytes 98308
  7.9 362.1 %copy-start.3 = (s32[32,256]{1,0:T(8,128)S(1)}, s32[32,256]{1,0:T(8,128)}, u32[]{:S(2)}) copy-start(s32[32,256]{1,0:T(8,128)} %param.10) | copy-start | bytes 98308
  7.9 362.1 %copy-start.4 = (s32[32,256]{1,0:T(8,128)S(1)}, s32[32,256]{1,0:T(8,128)}, u32[]{:S(2)}) copy-start(s32[32,256]{1,0:T(8,128)} %param.9) | copy-start | bytes 98308
  7.9 362.1 %all-reduce.3.cloned.1.call-start = ((), (), s32[]{:S(2)}) async-start(), calls=%async_computation.1 | async-start | bytes 2097152 | tf_op jit(solution)/shard_map/psum | solution.py:28
  82.2 355.4 %copy-start.1 = (bf16[256,768]{1,0:T(8,128)(2,1)S(1)}, bf16[256,768]{1,0:T(8,128)(2,1)}, u32[]{:S(2)}) copy-start(bf16[256,768]{1,0:T(8,128)(2,1)} %param.7) | copy-start | bytes 1179652
  85.4 352.2 %copy-start = (bf16[1024,768]{1,0:T(8,128)(2,1)S(1)}, bf16[1024,768]{1,0:T(8,128)(2,1)}, u32[]{:S(2)}) copy-start(bf16[1024,768]{1,0:T(8,128)(2,1)} %all-gather.2.cloned.1.call-done) | copy-start | bytes 4718596
  85.4 713.1 %all-reduce.5.cloned.1.call-start = ((), (), s32[]{:S(2)}) async-start(), calls=%async_computation.2 | async-start | bytes 2097152 | tf_op jit(solution)/shard_map/psum | solution.py:28
  437.6 79.2 %copy-start.5 = (f32[768]{0:T(1024)S(1)}, f32[768]{0:T(1024)}, u32[]{:S(2)}) copy-start(f32[768]{0:T(1024)} %param.11) | copy-start | bytes 9220
Sparse Core Ops, SparseCore 0:
  11.3 70.8 all-gather.1
  85.5 284.4 all-reduce.2
  518.6 279.8 all-reduce.4
where the time goes:
time: 953 us
  waiting for transfers between devices  639 us (67%)
  blocking collectives  291 us (31%)
  between operations  13.8 us (1%)
    psum x2, waiting for transfers between devices, local(): summed = lax.psum(partial_pred, 'vox')  565 us
    psum x2, blocking collectives, local(): gradient = lax.psum(local_grad, 'opt') * grad_scale  158 us
    all_gather x2, blocking collectives, local(): lax.all_gather(weighted_b, 'vox', axis=0, tiled=True)  133 us
    all_gather x1, waiting for transfers between devices, local(): lax.all_gather(source_fields, 'opt', axis=0, tiled=True)  74.2 us
  transfers between devices with their start and end apart: 3, of which 3 were waited for; matrix products, arithmetic and copies ran while one was open for 0% of the time, Pallas kernels for 0%

commit v1 on v0

--- a/solution.py
+++ b/solution.py
@@ -6,6 +6,13 @@
 NS = 1024
 ND = 4096
 ITERS = 2
+
+
+def swapped_in(x, axis, dim):
+    size = lax.axis_size(axis)
+    blocks = jnp.stack([x for _ in range(size)])
+    blocks = lax.all_to_all(blocks, axis, split_axis=0, concat_axis=0)
+    return jnp.concatenate(blocks, axis=dim)
 
 
 def local(source_fields, detector_fields, measured, valid_pair, weight_class, absorption):
@@ -20,7 +27,7 @@
     for step in range(ITERS):
         scaled = (detector_fields * mu_now[None, :]).astype(jnp.bfloat16)
         partial_pred = lax.dot_general(
-            lax.all_gather(source_fields, "opt", axis=0, tiled=True),
+            swapped_in(source_fields, "opt", 0),
             scaled,
             (((1,), (1,)), ((), ())),
             preferred_element_type=jnp.float32,

time: 953 us -> 940 us (0.986)
  waiting for transfers between devices: 639 us -> 583 us
  blocking collectives: 291 us -> 330 us
    all_gather x1, waiting for transfers between devices: 74.2 us -> 0.01 us  [local(): lax.all_gather(source_fields, 'opt', axis=0, tiled=True)]
    all_to_all x0 -> x1, blocking collectives: none -> 39.3 us  [swapped_in(): blocks = lax.all_to_all(blocks, axis, split_axis=0, concat_axis=0)]
    psum x2, waiting for transfers between devices: 565 us -> 583 us  [local(): summed = lax.psum(partial_pred, 'vox')]
  transfers between devices with their start and end apart: 3 -> 3, of which waited for: 3 -> 2; matrix products, arithmetic and copies ran while one was open for 0% -> 0% of each run, Pallas kernels for 0% -> 0%
where the time goes in v1:
time: 940 us
  waiting for transfers between devices  583 us (62%)
  blocking collectives  330 us (35%)
  between operations  15.6 us (2%)
    psum x2, waiting for transfers between devices, local(): summed = lax.psum(partial_pred, 'vox')  583 us
    psum x2, blocking collectives, local(): gradient = lax.psum(local_grad, 'opt') * grad_scale  158 us
    all_gather x2, blocking collectives, local(): lax.all_gather(weighted_b, 'vox', axis=0, tiled=True)  133 us
    all_to_all x1, blocking collectives, swapped_in(): blocks = lax.all_to_all(blocks, axis, split_axis=0, concat_axis=0)  39.3 us
  transfers between devices with their start and end apart: 3, of which 2 were waited for; matrix products, arithmetic and copies ran while one was open for 0% of the time, Pallas kernels for 0%

profile of v1, /device:TPU:1, one launch (start us, length us, event | category | flops | bytes accessed | tf_op | source)
XLA Modules:
  0.0 939.9 jit_solution(10117470338385089969)
XLA Ops:
  8.0 0.0 all-reduce.3.cloned.1.call-start
  8.0 1.0 stack.2
  9.1 0.0 copy-start
  9.1 0.0 copy-start.4
  9.1 39.3 %all_to_all.6 = bf16[16,64,768]{2,1,0:T(8,128)(2,1)S(1)} all-to-all(bf16[16,64,768]{2,1,0:T(8,128)(2,1)S(1)} %stack.2), channel_id=1, replica_groups=mesh['vox'=32,'opt'=16] {'opt'}, dimensions={0} | all-to-all | bytes 3145728 | tf_op jit(solution)/shard_map/all_to_all | solution.py:14
  48.4 0.0 copy-done
  48.4 0.0 copy-done.4
  48.4 0.0 copy-start.1
  48.4 0.0 copy-start.2
  48.4 0.0 copy-start.3
  48.4 1.6 convolution_bitcast_fusion.1
  50.0 0.0 all-reduce.3.cloned.1.call-update
  50.0 0.0 all-gather.2.cloned.1.call-start
  50.1 0.5 all-gather.2.cloned.1.call-update
  50.6 0.0 all-reduce.5.cloned.1.call-start
  50.7 302.6 %all-reduce.3.cloned.1.call-done = f32[1024,256]{1,0:T(8,128)} async-done(((f32[1024,256]{1,0:T(8,128)}), f32[1024,256]{1,0:T(8,128)}) %all-reduce.3.cloned.1.call-update) | async-done | bytes 1048592 | tf_op jit(solution)/shard_map/psum | solution.py:35
  353.3 0.0 copy-done.1
  353.3 0.0 copy-done.2
  353.3 0.0 copy-done.3
  353.3 0.8 multiply_convert_fusion
  354.1 66.8 %all_gather.10 = bf16[1024,256]{1,0:T(8,128)(2,1)S(1)} all-gather(bf16[32,256]{1,0:T(8,128)(2,1)S(1)} %multiply_convert_fusion), channel_id=1, replica_groups=mesh['vox'=32,'opt'=16] {'vox'}, dimensions={0}, use_global_device_ids=true | all-gather | bytes 540672 | tf_op jit(solution)/shard_map/all_gather | solution.py:40
  420.8 0.0 all-gather.2.cloned.1.call-done
  420.8 2.0 fusion
  422.9 78.6 %psum.29 = f32[768]{0:T(1024)S(1)} all-reduce(f32[768]{0:T(1024)S(1)} %fusion), channel_id=1, replica_groups=mesh['vox'=32,'opt'=16] {'opt'}, use_global_device_ids=true, to_apply=%region_2.0 | all-reduce | flops 768 | bytes 6144 | tf_op jit(solution)/shard_map/psum | solution.py:47
  501.5 1.6 convolution_bitcast_fusion
  503.1 0.0 all-reduce.5.cloned.1.call-update
  503.1 280.0 %all-reduce.5.cloned.1.call-done = f32[1024,256]{1,0:T(8,128)} async-done(((f32[1024,256]{1,0:T(8,128)}), f32[1024,256]{1,0:T(8,128)}) %all-reduce.5.cloned.1.call-update) | async-done | bytes 1048592 | tf_op jit(solution)/shard_map/psum | solution.py:35
  783.2 1.4 fusion.8
  784.5 65.8 %all_gather.12 = bf16[1024,256]{1,0:T(8,128)(2,1)S(1)} all-gather(bf16[32,256]{1,0:T(8,128)(2,1)S(1)} %get-tuple-element.6), channel_id=1, replica_groups=mesh['vox'=32,'opt'=16] {'vox'}, dimensions={0}, use_global_device_ids=true | all-gather | bytes 540672 | tf_op jit(solution)/shard_map/all_gather | solution.py:40
  850.4 2.0 fusion.1
  852.4 79.5 %psum.31 = f32[768]{0:T(1024)S(1)} all-reduce(f32[768]{0:T(1024)S(1)} %fusion.1), channel_id=1, replica_groups=mesh['vox'=32,'opt'=16] {'opt'}, use_global_device_ids=true, to_apply=%region_5.0 | all-reduce | flops 768 | bytes 6144 | tf_op jit(solution)/shard_map/psum | solution.py:47
  931.9 0.6 subtract_maximum_fusion
  (1 shorter events, 0.0 us)
Async XLA Ops:
  8.0 345.3 %all-reduce.3.cloned.1.call-start = ((), (), s32[]{:S(2)}) async-start(), calls=%async_computation.1 | async-start | bytes 2097152 | tf_op jit(solution)/shard_map/psum | solution.py:35
  9.1 39.3 %copy-start = (bf16[256,768]{1,0:T(8,128)(2,1)S(1)}, bf16[256,768]{1,0:T(8,128)(2,1)}, u32[]{:S(2)}) copy-start(bf16[256,768]{1,0:T(8,128)(2,1)} %param.7) | copy-start | bytes 1179652
  9.1 39.3 %copy-start.4 = (f32[768]{0:T(1024)S(1)}, f32[768]{0:T(1024)}, u32[]{:S(2)}) copy-start(f32[768]{0:T(1024)} %param.11) | copy-start | bytes 9220
  48.4 304.9 %copy-start.1 = (f32[32,256]{1,0:T(8,128)S(1)}, f32[32,256]{1,0:T(8,128)}, u32[]{:S(2)}) copy-start(f32[32,256]{1,0:T(8,128)} %param.8) | copy-start | bytes 98308
  48.4 304.9 %copy-start.2 = (s32[32,256]{1,0:T(8,128)S(1)}, s32[32,256]{1,0:T(8,128)}, u32[]{:S(2)}) copy-start(s32[32,256]{1,0:T(8,128)} %param.10) | copy-start | bytes 98308
  48.4 304.9 %copy-start.3 = (s32[32,256]{1,0:T(8,128)S(1)}, s32[32,256]{1,0:T(8,128)}, u32[]{:S(2)}) copy-start(s32[32,256]{1,0:T(8,128)} %param.9) | copy-start | bytes 98308
  50.0 370.8 %all-gather.2.cloned.1.call-start = ((), (), s32[]{:S(2)}) async-start(), calls=%async_computation.2 | async-start | bytes 1671168 | tf_op jit(solution)/shard_map/all_gather | solution.py:45
  50.6 732.5 %all-reduce.5.cloned.1.call-start = ((), (), s32[]{:S(2)}) async-start(), calls=%async_computation.3 | async-start | bytes 2097152 | tf_op jit(solution)/shard_map/psum | solution.py:35
Sparse Core Ops, SparseCore 0:
  50.2 303.0 all-reduce.2
  503.2 279.8 all-reduce.4
Sparse Core Ops, SparseCore 1:
  53.8 79.8 all-gather.1
